TPU v7x, 256 devices: a whole 4x4x8 slice. The times are simulated.
256 devices in a mesh: gx: 8 (over z), gy: 32 (over y, x, core).
Axes of the slice: x: 4, y: 4, z: 8, core: 2. Of those that a mesh axis runs over, the one named last changes fastest.
Arguments:
- ocean_field: float32 [16, 1024, 4096], P(None, 'gx', 'gy'), may hold values from -6 to 6
Outputs:
- detail_one: float32 [7, 8, 512, 2048], P(None, None, 'gx', 'gy')
- detail_two: float32 [7, 4, 256, 1024], P(None, None, 'gx', 'gy')
- detail_three: float32 [7, 2, 128, 512], P(None, None, 'gx', 'gy')
- approximation: float32 [2, 128, 512], P(None, 'gx', 'gy')
All inputs are finite; a program needn't handle non-finite values.
Results may differ from a plain program's by a relative error of at most 0.000022.
Values sent between devices are 32-bit elements; how exact they have to be, the bound alone decides.
A program may use at most 64 MiB of HBM per device.

v0:
```python
import jax
import jax.numpy as jnp
from jax import lax
from jax.sharding import PartitionSpec as P

LIFT_ALPHA = -1.586134342
LIFT_BETA = -0.05298011854
LIFT_GAMMA = 0.8829110762
LIFT_DELTA = 0.4435068522
LIFT_SCALE = 1.149604398
LIFT_INVERSE = 0.869864452


def passed_along(value, axis, steps):
    count = lax.axis_size(axis)
    pairs = [(source, (source + steps) % count) for source in range(count)]
    return lax.ppermute(value, axis, pairs)


def partner_2(value, axis, bit):
    mask = 2**bit
    pairs = [(source, source ^ mask) for source in range(lax.axis_size(axis))]
    return lax.ppermute(value, axis, pairs)


def split_pairs(blocks, axis_dim):
    shape = blocks.shape
    paired = blocks.reshape(shape[:axis_dim] + (shape[axis_dim] // 2, 2) + shape[axis_dim + 1 :])
    return (
        lax.index_in_dim(paired, 0, axis_dim + 1, False),
        lax.index_in_dim(paired, 1, axis_dim + 1, False),
    )


def lift_axis(blocks, axis_dim, next_even, prior_odd):
    even_part, odd_part = split_pairs(blocks, axis_dim)
    odd_part = odd_part + LIFT_ALPHA * (even_part + next_even(even_part))
    even_part = even_part + LIFT_BETA * (prior_odd(odd_part) + odd_part)
    odd_part = odd_part + LIFT_GAMMA * (even_part + next_even(even_part))
    even_part = even_part + LIFT_DELTA * (prior_odd(odd_part) + odd_part)
    stacked = jnp.stack([even_part * LIFT_SCALE, odd_part * LIFT_INVERSE])
    return stacked.reshape((2 * blocks.shape[0],) + stacked.shape[2:])


def mirror_lift(blocks):

    def next_even(values):
        return jnp.concatenate([values[:, 1:], values[:, -1:]], axis=1)

    def prior_odd(values):
        return jnp.concatenate([values[:, :1], values[:, :-1]], axis=1)

    return lift_axis(blocks, 1, next_even, prior_odd)


def wrap_lift(blocks, axis_dim):

    def next_even(values):
        return jnp.roll(values, -1, axis=axis_dim)

    def prior_odd(values):
        return jnp.roll(values, 1, axis=axis_dim)

    return lift_axis(blocks, axis_dim, next_even, prior_odd)


def trim_edges(values, axis_dim, margin):
    extent = values.shape[axis_dim]
    return lax.slice_in_dim(values, margin, extent - margin, axis=axis_dim)


def rim_lift(extended, axis_dim):
    return trim_edges(wrap_lift(extended, axis_dim), axis_dim, 2)


def step_lift_x(blocks):

    def next_even(values):
        extent = values.shape[2]
        first = lax.slice_in_dim(values, 0, 1, axis=2)
        return jnp.concatenate(
            [lax.slice_in_dim(values, 1, extent, axis=2), passed_along(first, "gx", -1)], axis=2
        )

    def prior_odd(values):
        extent = values.shape[2]
        final = lax.slice_in_dim(values, extent - 1, extent, axis=2)
        return jnp.concatenate(
            [passed_along(final, "gx", 1), lax.slice_in_dim(values, 0, extent - 1, axis=2)], axis=2
        )

    return lift_axis(blocks, 2, next_even, prior_odd)


def step_lift_y(blocks):

    def next_even(values):
        extent = values.shape[3]
        first = lax.slice_in_dim(values, 0, 1, axis=3)
        return jnp.concatenate(
            [lax.slice_in_dim(values, 1, extent, axis=3), passed_along(first, "gy", -1)], axis=3
        )

    def prior_odd(values):
        extent = values.shape[3]
        final = lax.slice_in_dim(values, extent - 1, extent, axis=3)
        return jnp.concatenate(
            [passed_along(final, "gy", 1), lax.slice_in_dim(values, 0, extent - 1, axis=3)], axis=3
        )

    return lift_axis(blocks, 3, next_even, prior_odd)


def fine_level(blocks):
    blocks = step_lift_x(blocks)
    blocks = step_lift_y(blocks)
    return mirror_lift(blocks)


def coarse_lift_x(blocks):
    extent = blocks.shape[2]
    upper = passed_along(lax.slice_in_dim(blocks, extent - 4, extent, axis=2), "gx", 2)
    lower = passed_along(lax.slice_in_dim(blocks, 0, 4, axis=2), "gx", -2)
    return rim_lift(jnp.concatenate([upper, blocks, lower], axis=2), 2)


def coarse_lift_y(blocks):
    extent = blocks.shape[3]
    upper = passed_along(lax.slice_in_dim(blocks, extent - 4, extent, axis=3), "gy", 2)
    lower = passed_along(lax.slice_in_dim(blocks, 0, 4, axis=3), "gy", -2)
    return rim_lift(jnp.concatenate([upper, blocks, lower], axis=3), 3)


def coarse_level(blocks):
    blocks = coarse_lift_x(blocks)
    blocks = coarse_lift_y(blocks)
    return mirror_lift(blocks)


def take_quarter(values, parity_x, parity_y):
    rows_half = values.shape[2] // 2
    cols_half = values.shape[3] // 2
    values = lax.dynamic_slice_in_dim(values, parity_x * rows_half, rows_half, 2)
    return lax.dynamic_slice_in_dim(values, parity_y * cols_half, cols_half, 3)


def shards(ocean_field):
    blocks = fine_level(ocean_field[None])
    detail_one = blocks[1:]
    low_band = blocks[:1]
    parity_x = lax.axis_index("gx") % 2
    parity_y = lax.axis_index("gy") % 2
    partner = partner_2(low_band, "gx", 0)
    joined = jnp.where(
        parity_x == 0,
        jnp.concatenate([low_band, partner], axis=2),
        jnp.concatenate([partner, low_band], axis=2),
    )
    partner = partner_2(joined, "gy", 0)
    joined = jnp.where(
        parity_y == 0,
        jnp.concatenate([joined, partner], axis=3),
        jnp.concatenate([partner, joined], axis=3),
    )
    blocks = coarse_level(joined)
    detail_two = take_quarter(blocks[1:], parity_x, parity_y)
    blocks = coarse_level(blocks[:1])
    detail_three = take_quarter(blocks[1:], parity_x, parity_y)
    approximation = take_quarter(blocks[:1], parity_x, parity_y)[0]
    return (detail_one, detail_two, detail_three, approximation)


def solution(mesh):
    placed = (P(None, "gx", "gy"),)
    return jax.shard_map(
        shards,
        mesh=mesh,
        in_specs=placed,
        out_specs=(
            P(None, None, "gx", "gy"),
            P(None, None, "gx", "gy"),
            P(None, None, "gx", "gy"),
            P(None, "gx", "gy"),
        ),
        check_vma=False,
    )
```

profile of v0, /device:TPU:94, one launch (start us, length us, event | category | flops | bytes accessed | tf_op | source)
XLA Modules:
  0.0 134.7 jit_solution(1403559729054361365)
XLA Ops:
  0.6 1.8 %copy.390 = f32[16,128,128]{2,0,1:T(8,128)S(1)} copy(f32[16,128,128]{2,1,0:T(8,128)} %param.1) | data formatting | bytes 2097152 | tf_op args[0]
  3.5 3.5 %collective-permute-done = f32[1,16,1,128]{3,1,2,0:T(8,128)S(1)} collective-permute-done((f32[1,16,1,128]{3,1,2,0:T(8,128)S(1)}, f32[1,16,1,128]{3,1,2,0:T(8,128)S(1)}, u32[]{:S(2)}, u32[]{:S(2)}) %collective-permute-start) | collective-permute-done | bytes 8224 | tf_op jit(solution)/shard_map/ppermute | solution.py:17
  7.2 3.2 %collective-permute-start.1 = (f32[1,16,1,128]{3,1,2,0:T(8,128)S(1)}, f32[1,16,1,128]{3,1,2,0:T(8,128)S(1)}, u32[]{:S(2)}, u32[]{:S(2)}) collective-permute-start(f32[1,16,1,128]{3,1,2,0:T(8,128)S(1)} %slice.446), channel_id=1, source_target_pairs={{0,32},{32,64},{64,96},{96,128},{128,160},{160,192},{192,224},{224... | collective-permute-start | bytes 24584 | tf_op jit(solution)/shard_map/ppermute | solution.py:17
  12.9 3.0 %collective-permute-done.2 = f32[1,16,1,128]{3,1,2,0:T(8,128)S(1)} collective-permute-done((f32[1,16,1,128]{3,1,2,0:T(8,128)S(1)}, f32[1,16,1,128]{3,1,2,0:T(8,128)S(1)}, u32[]{:S(2)}, u32[]{:S(2)}) %collective-permute-start.2) | collective-permute-done | bytes 8224 | tf_op jit(solution)/shard_map/ppermute | solution.py:17
  16.8 3.2 %collective-permute-start.3 = (f32[1,16,1,128]{3,1,2,0:T(8,128)S(1)}, f32[1,16,1,128]{3,1,2,0:T(8,128)S(1)}, u32[]{:S(2)}, u32[]{:S(2)}) collective-permute-start(f32[1,16,1,128]{3,1,2,0:T(8,128)S(1)} %slice.450), channel_id=1, source_target_pairs={{0,32},{32,64},{64,96},{96,128},{128,160},{160,192},{192,224},{224... | collective-permute-start | bytes 24584 | tf_op jit(solution)/shard_map/ppermute | solution.py:17
  20.6 2.5 %copy.392 = f32[1,16,64,1,128]{2,1,4,3,0:T(8,128)} copy(f32[1,16,64,1,128]{4,1,2,3,0:T(8,128)} %get-tuple-element.46) | data formatting | bytes 1048576 | tf_op jit(solution)/shard_map/slice | solution.py:30
  26.2 1.8 %copy.399 = f32[1,16,1,64,2]{2,1,4,3,0:T(8,128)} copy(f32[1,16,1,64,2]{1,4,3,2,0:T(2,128)S(1)} %bitcast.440) | data formatting | bytes 16384 | tf_op jit(solution)/shard_map/concatenate | solution.py:81
  29.6 1.8 %copy.395 = f32[1,16,1,64,2]{2,1,4,3,0:T(8,128)} copy(f32[1,16,1,64,2]{1,4,3,2,0:T(2,128)S(1)} %bitcast.441) | data formatting | bytes 16384 | tf_op jit(solution)/shard_map/concatenate | solution.py:88
  32.2 2.7 %copy.401 = f32[1,16,63,128]{2,1,3,0:T(8,128)} copy(f32[1,16,63,128]{3,1,2,0:T(8,128)} %slice.451) | data formatting | bytes 1032192 | tf_op jit(solution)/shard_map/slice | solution.py:89
  35.0 1.8 %copy.405 = f32[1,16,1,64,2]{2,1,4,3,0:T(8,128)} copy(f32[1,16,1,64,2]{1,4,3,2,0:T(2,128)S(1)} %bitcast.442) | data formatting | bytes 16384 | tf_op jit(solution)/shard_map/concatenate | solution.py:81
  36.9 1.9 %copy.402 = f32[1,16,1,64,2]{2,1,4,3,0:T(8,128)} copy(f32[1,16,1,64,2]{1,4,3,2,0:T(2,128)S(1)} %bitcast.443) | data formatting | bytes 16384 | tf_op jit(solution)/shard_map/concatenate | solution.py:88
  38.8 4.4 %broadcast_multiply_fusion.2 = (f32[1,16,64,64,2]{2,1,4,3,0:T(8,128)S(1)}, f32[1,16,64,64,2]{2,1,4,3,0:T(8,128)S(1)}) fusion(f32[1,16,1,64,2]{2,1,4,3,0:T(8,128)} %copy.405, f32[1,16,63,64,2]{2,1,4,3,0:T(8,128)} %bitcast.422, f32[1,16,64,64,2]{2,1,4,3,0:T(8,128)S(1)} %bitcast.419, f32[1,16,63,64,2]{2,1,4,3,0:T(8,128)} %bitcast.421, ...), kind=kLoop, calls=%fused_computation.131 | loop fusion | flops 2359296 | bytes 4194304 | tf_op jit(solution)/shard_map/mul | solution.py:41
  45.2 1.6 %collective-permute-start.5 = (f32[2,16,64,1]{2,1,3,0:T(8,128)S(1)}, f32[2,16,64,1]{2,1,3,0:T(8,128)S(1)}, u32[]{:S(2)}, u32[]{:S(2)}) collective-permute-start(f32[2,16,64,1]{2,1,3,0:T(8,128)S(1)} %slice.456), channel_id=1, source_target_pairs={{0,1},{1,2},{2,3},{3,4},{4,5},{5,6},{6,7},{7,8},{8,9},{9,10},{10,1... | collective-permute-start | bytes 24584 | tf_op jit(solution)/shard_map/ppermute | solution.py:17
  47.0 1.7 %collective-permute-done.5 = f32[2,16,64,1]{2,1,3,0:T(8,128)S(1)} collective-permute-done((f32[2,16,64,1]{2,1,3,0:T(8,128)S(1)}, f32[2,16,64,1]{2,1,3,0:T(8,128)S(1)}, u32[]{:S(2)}, u32[]{:S(2)}) %collective-permute-start.5) | collective-permute-done | bytes 8224 | tf_op jit(solution)/shard_map/ppermute | solution.py:17
  50.6 4.7 %collective-permute-start.7 = (f32[2,16,64,1]{2,1,3,0:T(8,128)S(1)}, f32[2,16,64,1]{2,1,3,0:T(8,128)S(1)}, u32[]{:S(2)}, u32[]{:S(2)}) collective-permute-start(f32[2,16,64,1]{2,1,3,0:T(8,128)S(1)} %slice.460), channel_id=1, source_target_pairs={{0,1},{1,2},{2,3},{3,4},{4,5},{5,6},{6,7},{7,8},{8,9},{9,10},{10,1... | collective-permute-start | bytes 24584 | tf_op jit(solution)/shard_map/ppermute | solution.py:17
  58.5 2.1 %copy.414 = f32[2,2,16,64,64]{4,3,2,1,0:T(8,128)S(1)} copy(f32[2,2,16,64,64]{3,2,4,1,0:T(8,128)} %pad_maximum_fusion) | data formatting | bytes 2097152 | tf_op jit(solution)/shard_map/stack | solution.py:41
  63.8 1.8 %collective-permute-start.8 = (f32[1,8,64,64]{3,1,2,0:T(8,128)S(1)}, f32[1,8,64,64]{3,1,2,0:T(8,128)S(1)}, u32[]{:S(2)}, u32[]{:S(2)}) collective-permute-start(f32[1,8,64,64]{3,1,2,0:T(8,128)S(1)} %copy.489), channel_id=1, source_target_pairs={{0,32},{32,0},{64,96},{96,64},{128,160},{160,128},{192,224},{224,1... | collective-permute-start | bytes 393224 | tf_op jit(solution)/shard_map/ppermute | solution.py:23
  65.6 6.8 %collective-permute-done.8 = f32[1,8,64,64]{3,1,2,0:T(8,128)S(1)} collective-permute-done((f32[1,8,64,64]{3,1,2,0:T(8,128)S(1)}, f32[1,8,64,64]{3,1,2,0:T(8,128)S(1)}, u32[]{:S(2)}, u32[]{:S(2)}) %collective-permute-start.8) | collective-permute-done | bytes 131104 | tf_op jit(solution)/shard_map/ppermute | solution.py:23
  73.3 2.1 %collective-permute-done.9 = f32[1,8,128,64]{3,1,2,0:T(8,128)S(1)} collective-permute-done((f32[1,8,128,64]{3,1,2,0:T(8,128)}, f32[1,8,128,64]{3,1,2,0:T(8,128)S(1)}, u32[]{:S(2)}, u32[]{:S(2)}) %collective-permute-start.9) | collective-permute-done | bytes 262176 | tf_op jit(solution)/shard_map/ppermute | solution.py:23
  75.7 1.5 %collective-permute-start.10 = (f32[1,8,4,128]{3,1,2,0:T(8,128)S(1)}, f32[1,8,4,128]{3,1,2,0:T(8,128)S(1)}, u32[]{:S(2)}, u32[]{:S(2)}) collective-permute-start(f32[1,8,4,128]{3,1,2,0:T(8,128)S(1)} %get-tuple-element.73), channel_id=1, source_target_pairs={{0,64},{32,96},{64,128},{96,160},{128,192},{160,224},{192,0},{224,... | collective-permute-start | bytes 49160 | tf_op jit(solution)/shard_map/ppermute | solution.py:17
  78.7 1.7 %collective-permute-done.10 = f32[1,8,4,128]{3,1,2,0:T(8,128)S(1)} collective-permute-done((f32[1,8,4,128]{3,1,2,0:T(8,128)S(1)}, f32[1,8,4,128]{3,1,2,0:T(8,128)S(1)}, u32[]{:S(2)}, u32[]{:S(2)}) %collective-permute-start.10) | collective-permute-done | bytes 16416 | tf_op jit(solution)/shard_map/ppermute | solution.py:17
  80.5 2.7 %collective-permute-done.11 = f32[1,8,4,128]{3,1,2,0:T(8,128)S(1)} collective-permute-done((f32[1,8,4,128]{3,1,2,0:T(8,128)S(1)}, f32[1,8,4,128]{3,1,2,0:T(8,128)S(1)}, u32[]{:S(2)}, u32[]{:S(2)}) %collective-permute-start.11) | collective-permute-done | bytes 16416 | tf_op jit(solution)/shard_map/ppermute | solution.py:17
  84.0 3.4 %collective-permute-start.12 = (f32[2,8,64,4]{3,1,2,0:T(8,128)S(1)}, f32[2,8,64,4]{3,1,2,0:T(8,128)S(1)}, u32[]{:S(2)}, u32[]{:S(2)}) collective-permute-start(f32[2,8,64,4]{3,1,2,0:T(8,128)S(1)} %get-tuple-element.59), channel_id=1, source_target_pairs={{0,2},{1,3},{2,4},{3,5},{4,6},{5,7},{6,8},{7,9},{8,10},{9,11},{10,... | collective-permute-start | bytes 49160 | tf_op jit(solution)/shard_map/ppermute | solution.py:17
  87.5 10.0 %collective-permute-done.12 = f32[2,8,64,4]{3,1,2,0:T(8,128)S(1)} collective-permute-done((f32[2,8,64,4]{3,1,2,0:T(8,128)S(1)}, f32[2,8,64,4]{3,1,2,0:T(8,128)S(1)}, u32[]{:S(2)}, u32[]{:S(2)}) %collective-permute-start.12) | collective-permute-done | bytes 16416 | tf_op jit(solution)/shard_map/ppermute | solution.py:17
  97.5 5.5 %collective-permute-done.13 = f32[2,8,64,4]{3,1,2,0:T(8,128)S(1)} collective-permute-done((f32[2,8,64,4]{3,1,2,0:T(8,128)S(1)}, f32[2,8,64,4]{3,1,2,0:T(8,128)S(1)}, u32[]{:S(2)}, u32[]{:S(2)}) %collective-permute-start.13) | collective-permute-done | bytes 16416 | tf_op jit(solution)/shard_map/ppermute | solution.py:17
  104.5 1.8 %copy.422 = f32[2,8,64,136]{2,1,3,0:T(8,128)S(1)} copy(f32[2,8,64,136]{3,1,2,0:T(8,128)} %pad_maximum_fusion.4) | data formatting | bytes 1114112 | tf_op jit(solution)/shard_map/concatenate | solution.py:131
  108.8 1.6 %slice.499 = f32[4,8,64,64]{3,2,1,0:T(8,128)S(1)} slice(f32[4,8,64,68]{3,2,1,0:T(8,128)} %bitcast.424), slice={[0:4], [0:8], [0:64], [2:66]} | slice | bytes 1048576 | tf_op jit(solution)/shard_map/slice | solution.py:69
  111.8 2.4 %collective-permute-start.14 = (f32[1,4,4,64]{3,2,1,0:T(4,128)S(1)}, f32[1,4,4,64]{3,2,1,0:T(4,128)S(1)}, u32[]{:S(2)}, u32[]{:S(2)}) collective-permute-start(f32[1,4,4,64]{3,2,1,0:T(4,128)S(1)} %get-tuple-element.24), channel_id=1, source_target_pairs={{0,64},{32,96},{64,128},{96,160},{128,192},{160,224},{192,0},{224,... | collective-permute-start | bytes 12296 | tf_op jit(solution)/shard_map/ppermute | solution.py:17
  116.5 3.5 %collective-permute-done.15 = f32[1,4,4,64]{3,2,1,0:T(4,128)S(1)} collective-permute-done((f32[1,4,4,64]{3,2,1,0:T(4,128)S(1)}, f32[1,4,4,64]{3,2,1,0:T(4,128)S(1)}, u32[]{:S(2)}, u32[]{:S(2)}) %collective-permute-start.15) | collective-permute-done | bytes 4128 | tf_op jit(solution)/shard_map/ppermute | solution.py:17
  122.4 1.7 %collective-permute-start.17 = (f32[2,4,32,4]{3,0,2,1:T(2,128)S(1)}, f32[2,4,32,4]{3,0,2,1:T(2,128)S(1)}, u32[]{:S(2)}, u32[]{:S(2)}) collective-permute-start(f32[2,4,32,4]{3,0,2,1:T(2,128)S(1)} %get-tuple-element.96), channel_id=1, source_target_pairs={{0,30},{1,31},{2,0},{3,1},{4,2},{5,3},{6,4},{7,5},{8,6},{9,7},{10,... | collective-permute-start | bytes 12296 | tf_op jit(solution)/shard_map/ppermute | solution.py:17
  125.1 2.0 %collective-permute-done.16 = f32[2,4,32,4]{3,0,2,1:T(2,128)S(1)} collective-permute-done((f32[2,4,32,4]{3,0,2,1:T(2,128)S(1)}, f32[2,4,32,4]{3,0,2,1:T(2,128)S(1)}, u32[]{:S(2)}, u32[]{:S(2)}) %collective-permute-start.16) | collective-permute-done | bytes 4128 | tf_op jit(solution)/shard_map/ppermute | solution.py:17
  127.1 3.6 %collective-permute-done.17 = f32[2,4,32,4]{3,0,2,1:T(2,128)S(1)} collective-permute-done((f32[2,4,32,4]{3,0,2,1:T(2,128)S(1)}, f32[2,4,32,4]{3,0,2,1:T(2,128)S(1)}, u32[]{:S(2)}, u32[]{:S(2)}) %collective-permute-start.17) | collective-permute-done | bytes 4128 | tf_op jit(solution)/shard_map/ppermute | solution.py:17
  (183 shorter events, 39.3 us)
Async XLA Ops:
  3.4 3.7 %collective-permute-start = (f32[1,16,1,128]{3,1,2,0:T(8,128)S(1)}, f32[1,16,1,128]{3,1,2,0:T(8,128)S(1)}, u32[]{:S(2)}, u32[]{:S(2)}) collective-permute-start(f32[1,16,1,128]{3,1,2,0:T(8,128)S(1)} %slice.445), channel_id=1, source_target_pairs={{0,224},{32,0},{64,32},{96,64},{128,96},{160,128},{192,160},{224,1... | collective-permute-start | bytes 24584 | tf_op jit(solution)/shard_map/ppermute | solution.py:17
  7.2 4.6 %collective-permute-start.1 = (f32[1,16,1,128]{3,1,2,0:T(8,128)S(1)}, f32[1,16,1,128]{3,1,2,0:T(8,128)S(1)}, u32[]{:S(2)}, u32[]{:S(2)}) collective-permute-start(f32[1,16,1,128]{3,1,2,0:T(8,128)S(1)} %slice.446), channel_id=1, source_target_pairs={{0,32},{32,64},{64,96},{96,128},{128,160},{160,192},{192,224},{224... | collective-permute-start | bytes 24584 | tf_op jit(solution)/shard_map/ppermute | solution.py:17
  11.9 4.0 %collective-permute-start.2 = (f32[1,16,1,128]{3,1,2,0:T(8,128)S(1)}, f32[1,16,1,128]{3,1,2,0:T(8,128)S(1)}, u32[]{:S(2)}, u32[]{:S(2)}) collective-permute-start(f32[1,16,1,128]{3,1,2,0:T(8,128)S(1)} %slice.449), channel_id=1, source_target_pairs={{0,224},{32,0},{64,32},{96,64},{128,96},{160,128},{192,160},{224,1... | collective-permute-start | bytes 24584 | tf_op jit(solution)/shard_map/ppermute | solution.py:17
  16.0 0.8 copy-start.2
  16.8 20.0 %collective-permute-start.3 = (f32[1,16,1,128]{3,1,2,0:T(8,128)S(1)}, f32[1,16,1,128]{3,1,2,0:T(8,128)S(1)}, u32[]{:S(2)}, u32[]{:S(2)}) collective-permute-start(f32[1,16,1,128]{3,1,2,0:T(8,128)S(1)} %slice.450), channel_id=1, source_target_pairs={{0,32},{32,64},{64,96},{96,128},{128,160},{160,192},{192,224},{224... | collective-permute-start | bytes 24584 | tf_op jit(solution)/shard_map/ppermute | solution.py:17
  26.1 5.3 %copy-start.3 = (f32[1,16,64,128]{3,1,2,0:T(8,128)S(1)}, f32[1,16,64,128]{3,1,2,0:T(8,128)}, u32[]{:S(2)}) copy-start(f32[1,16,64,128]{3,1,2,0:T(8,128)} %copy-done.2) | copy-start | bytes 1572868
  32.2 6.6 %copy-start = (f32[1,16,64,1,128]{2,1,4,3,0:T(8,128)S(1)}, f32[1,16,64,1,128]{2,1,4,3,0:T(8,128)}, u32[]{:S(2)}) copy-start(f32[1,16,64,1,128]{2,1,4,3,0:T(8,128)} %copy.392) | copy-start | bytes 1572868
  32.2 6.6 %copy-start.1 = (f32[1,16,64,1,128]{2,1,4,3,0:T(8,128)S(1)}, f32[1,16,64,1,128]{2,1,4,3,0:T(8,128)}, u32[]{:S(2)}) copy-start(f32[1,16,64,1,128]{2,1,4,3,0:T(8,128)} %copy.396) | copy-start | bytes 1572868
  43.4 1.5 %collective-permute-start.4 = (f32[2,16,64,1]{2,1,3,0:T(8,128)S(1)}, f32[2,16,64,1]{2,1,3,0:T(8,128)S(1)}, u32[]{:S(2)}, u32[]{:S(2)}) collective-permute-start(f32[2,16,64,1]{2,1,3,0:T(8,128)S(1)} %slice.455), channel_id=1, source_target_pairs={{0,31},{1,0},{2,1},{3,2},{4,3},{5,4},{6,5},{7,6},{8,7},{9,8},{10,9... | collective-permute-start | bytes 24584 | tf_op jit(solution)/shard_map/ppermute | solution.py:17
  45.2 3.4 %collective-permute-start.5 = (f32[2,16,64,1]{2,1,3,0:T(8,128)S(1)}, f32[2,16,64,1]{2,1,3,0:T(8,128)S(1)}, u32[]{:S(2)}, u32[]{:S(2)}) collective-permute-start(f32[2,16,64,1]{2,1,3,0:T(8,128)S(1)} %slice.456), channel_id=1, source_target_pairs={{0,1},{1,2},{2,3},{3,4},{4,5},{5,6},{6,7},{7,8},{8,9},{9,10},{10,1... | collective-permute-start | bytes 24584 | tf_op jit(solution)/shard_map/ppermute | solution.py:17
  48.9 1.5 %collective-permute-start.6 = (f32[2,16,64,1]{2,1,3,0:T(8,128)S(1)}, f32[2,16,64,1]{2,1,3,0:T(8,128)S(1)}, u32[]{:S(2)}, u32[]{:S(2)}) collective-permute-start(f32[2,16,64,1]{2,1,3,0:T(8,128)S(1)} %slice.459), channel_id=1, source_target_pairs={{0,31},{1,0},{2,1},{3,2},{4,3},{5,4},{6,5},{7,6},{8,7},{9,8},{10,9... | collective-permute-start | bytes 24584 | tf_op jit(solution)/shard_map/ppermute | solution.py:17
  50.6 5.6 %collective-permute-start.7 = (f32[2,16,64,1]{2,1,3,0:T(8,128)S(1)}, f32[2,16,64,1]{2,1,3,0:T(8,128)S(1)}, u32[]{:S(2)}, u32[]{:S(2)}) collective-permute-start(f32[2,16,64,1]{2,1,3,0:T(8,128)S(1)} %slice.460), channel_id=1, source_target_pairs={{0,1},{1,2},{2,3},{3,4},{4,5},{5,6},{6,7},{7,8},{8,9},{9,10},{10,1... | collective-permute-start | bytes 24584 | tf_op jit(solution)/shard_map/ppermute | solution.py:17
  63.8 8.6 %collective-permute-start.8 = (f32[1,8,64,64]{3,1,2,0:T(8,128)S(1)}, f32[1,8,64,64]{3,1,2,0:T(8,128)S(1)}, u32[]{:S(2)}, u32[]{:S(2)}) collective-permute-start(f32[1,8,64,64]{3,1,2,0:T(8,128)S(1)} %copy.489), channel_id=1, source_target_pairs={{0,32},{32,0},{64,96},{96,64},{128,160},{160,128},{192,224},{224,1... | collective-permute-start | bytes 393224 | tf_op jit(solution)/shard_map/ppermute | solution.py:23
  73.3 2.1 %collective-permute-start.9 = (f32[1,8,128,64]{3,1,2,0:T(8,128)}, f32[1,8,128,64]{3,1,2,0:T(8,128)S(1)}, u32[]{:S(2)}, u32[]{:S(2)}) collective-permute-start(f32[1,8,128,64]{3,1,2,0:T(8,128)} %maximum_select_fusion.1), channel_id=1, source_target_pairs={{0,1},{1,0},{2,3},{3,2},{4,5},{5,4},{6,7},{7,6},{8,9},{9,8},{10,11... | collective-permute-start | bytes 786440 | tf_op jit(solution)/shard_map/ppermute | solution.py:23
  75.7 4.7 %collective-permute-start.10 = (f32[1,8,4,128]{3,1,2,0:T(8,128)S(1)}, f32[1,8,4,128]{3,1,2,0:T(8,128)S(1)}, u32[]{:S(2)}, u32[]{:S(2)}) collective-permute-start(f32[1,8,4,128]{3,1,2,0:T(8,128)S(1)} %get-tuple-element.73), channel_id=1, source_target_pairs={{0,64},{32,96},{64,128},{96,160},{128,192},{160,224},{192,0},{224,... | collective-permute-start | bytes 49160 | tf_op jit(solution)/shard_map/ppermute | solution.py:17
  77.3 5.8 %collective-permute-start.11 = (f32[1,8,4,128]{3,1,2,0:T(8,128)S(1)}, f32[1,8,4,128]{3,1,2,0:T(8,128)S(1)}, u32[]{:S(2)}, u32[]{:S(2)}) collective-permute-start(f32[1,8,4,128]{3,1,2,0:T(8,128)S(1)} %get-tuple-element.74), channel_id=1, source_target_pairs={{0,192},{32,224},{64,0},{96,32},{128,64},{160,96},{192,128},{224,1... | collective-permute-start | bytes 49160 | tf_op jit(solution)/shard_map/ppermute | solution.py:17
  84.0 13.5 %collective-permute-start.12 = (f32[2,8,64,4]{3,1,2,0:T(8,128)S(1)}, f32[2,8,64,4]{3,1,2,0:T(8,128)S(1)}, u32[]{:S(2)}, u32[]{:S(2)}) collective-permute-start(f32[2,8,64,4]{3,1,2,0:T(8,128)S(1)} %get-tuple-element.59), channel_id=1, source_target_pairs={{0,2},{1,3},{2,4},{3,5},{4,6},{5,7},{6,8},{7,9},{8,10},{9,11},{10,... | collective-permute-start | bytes 49160 | tf_op jit(solution)/shard_map/ppermute | solution.py:17
  87.5 15.6 %collective-permute-start.13 = (f32[2,8,64,4]{3,1,2,0:T(8,128)S(1)}, f32[2,8,64,4]{3,1,2,0:T(8,128)S(1)}, u32[]{:S(2)}, u32[]{:S(2)}) collective-permute-start(f32[2,8,64,4]{3,1,2,0:T(8,128)S(1)} %get-tuple-element.60), channel_id=1, source_target_pairs={{0,30},{1,31},{2,0},{3,1},{4,2},{5,3},{6,4},{7,5},{8,6},{9,7},{10,... | collective-permute-start | bytes 49160 | tf_op jit(solution)/shard_map/ppermute | solution.py:17
  111.8 4.6 %collective-permute-start.14 = (f32[1,4,4,64]{3,2,1,0:T(4,128)S(1)}, f32[1,4,4,64]{3,2,1,0:T(4,128)S(1)}, u32[]{:S(2)}, u32[]{:S(2)}) collective-permute-start(f32[1,4,4,64]{3,2,1,0:T(4,128)S(1)} %get-tuple-element.24), channel_id=1, source_target_pairs={{0,64},{32,96},{64,128},{96,160},{128,192},{160,224},{192,0},{224,... | collective-permute-start | bytes 12296 | tf_op jit(solution)/shard_map/ppermute | solution.py:17
  114.2 5.8 %collective-permute-start.15 = (f32[1,4,4,64]{3,2,1,0:T(4,128)S(1)}, f32[1,4,4,64]{3,2,1,0:T(4,128)S(1)}, u32[]{:S(2)}, u32[]{:S(2)}) collective-permute-start(f32[1,4,4,64]{3,2,1,0:T(4,128)S(1)} %get-tuple-element.25), channel_id=1, source_target_pairs={{0,192},{32,224},{64,0},{96,32},{128,64},{160,96},{192,128},{224,1... | collective-permute-start | bytes 12296 | tf_op jit(solution)/shard_map/ppermute | solution.py:17
  122.0 5.0 %collective-permute-start.16 = (f32[2,4,32,4]{3,0,2,1:T(2,128)S(1)}, f32[2,4,32,4]{3,0,2,1:T(2,128)S(1)}, u32[]{:S(2)}, u32[]{:S(2)}) collective-permute-start(f32[2,4,32,4]{3,0,2,1:T(2,128)S(1)} %get-tuple-element.95), channel_id=1, source_target_pairs={{0,2},{1,3},{2,4},{3,5},{4,6},{5,7},{6,8},{7,9},{8,10},{9,11},{10,... | collective-permute-start | bytes 12296 | tf_op jit(solution)/shard_map/ppermute | solution.py:17
  122.4 8.3 %collective-permute-start.17 = (f32[2,4,32,4]{3,0,2,1:T(2,128)S(1)}, f32[2,4,32,4]{3,0,2,1:T(2,128)S(1)}, u32[]{:S(2)}, u32[]{:S(2)}) collective-permute-start(f32[2,4,32,4]{3,0,2,1:T(2,128)S(1)} %get-tuple-element.96), channel_id=1, source_target_pairs={{0,30},{1,31},{2,0},{3,1},{4,2},{5,3},{6,4},{7,5},{8,6},{9,7},{10,... | collective-permute-start | bytes 12296 | tf_op jit(solution)/shard_map/ppermute | solution.py:17
where the time goes:
time: 135 us
  waiting for transfers between devices  50.8 us (38%)
  local copies, waits for them, and re-layouts  37.3 us (28%)
  starting transfers between devices  27.4 us (20%)
  other arithmetic  17.5 us (13%)
  between operations  1.65 us (1%)
    ppermute x16, waiting for transfers between devices, passed_along(): return lax.ppermute(value, axis, pairs)  42 us
    ppermute x16, starting transfers between devices, passed_along(): return lax.ppermute(value, axis, pairs)  25.6 us
    ppermute x2, waiting for transfers between devices, partner_2(): return lax.ppermute(value, axis, pairs)  8.87 us
    mul x10, other arithmetic, lift_axis(): stacked = jnp.stack([even_part * LIFT_SCALE, odd_part * LIFT_INVERSE])  7.76 us
    slice x4, local copies, waits for them, and re-layouts, prior_odd(): lax.slice_in_dim(values, 0, extent - 1, axis=2)  5.08 us
    concatenate x2, local copies, waits for them, and re-layouts, prior_odd(): jnp.concatenate([passed_along(final, 'gx', 1), lax.slice_in_dim(values, 0...  3.68 us
    concatenate x2, local copies, waits for them, and re-layouts, next_even(): jnp.concatenate([lax.slice_in_dim(values, 1, extent, axis=2), passed_alon...  3.6 us
    another operation x2, local copies, waits for them, and re-layouts, lift_axis(): stacked = jnp.stack([even_part * LIFT_SCALE, odd_part * LIFT_INVERSE])  3.46 us
  transfers between devices with their start and end apart: 18, of which 17 were waited for; matrix products, arithmetic and copies ran while one was open for 15% of the time, Pallas kernels for 0%

commit v1 on v0

v1 whole, which is shorter than its diff:
```python
import functools

import jax
import jax.numpy as jnp
import numpy as np
from jax import lax
from jax.experimental import pallas as pl
from jax.experimental.pallas import tpu as pltpu
from jax.sharding import PartitionSpec as P

LIFT_ALPHA = -1.586134342
LIFT_BETA = -0.05298011854
LIFT_GAMMA = 0.8829110762
LIFT_DELTA = 0.4435068522
LIFT_SCALE = 1.149604398
LIFT_INVERSE = 0.869864452

MESH = pl.DeviceIdType.MESH
N = 128
TOP = 32
EXT = 192
LEFT, RIGHT, HIGH, PLANES = 8, 11, 14, 22
DEEP = 13


def lift_matrix(extent):
    v = np.eye(extent)
    s, d = v[0::2], v[1::2]
    d = d + LIFT_ALPHA * (s + np.roll(s, -1, 0))
    s = s + LIFT_BETA * (np.roll(d, 1, 0) + d)
    d = d + LIFT_GAMMA * (s + np.roll(s, -1, 0))
    s = s + LIFT_DELTA * (np.roll(d, 1, 0) + d)
    return LIFT_SCALE * s, LIFT_INVERSE * d


def lane_filters():
    low1, high1 = lift_matrix(2 * N)
    low2, high2 = lift_matrix(N)
    low3, high3 = lift_matrix(N // 2)
    one = np.concatenate([low1[: N // 2], high1[: N // 2]]).T
    two = np.concatenate([(low2 @ low1)[: N // 4], (high2 @ low1)[: N // 4]]).T
    three = np.concatenate([(low3 @ low2 @ low1)[: N // 8], (high3 @ low2 @ low1)[: N // 8]]).T
    pad = lambda w: np.pad(w, ((0, 0), (0, N - w.shape[1]))).astype(np.float32)
    return np.stack([pad(one), pad(two), pad(three)])


def mirror_lift(planes):
    count = len(planes) // 2
    s, d = list(planes[0::2]), list(planes[1::2])
    after = lambda v, n: v[min(n + 1, count - 1)]
    before = lambda v, n: v[max(n - 1, 0)]
    d = [d[n] + LIFT_ALPHA * (s[n] + after(s, n)) for n in range(count)]
    s = [s[n] + LIFT_BETA * (before(d, n) + d[n]) for n in range(count)]
    d = [d[n] + LIFT_GAMMA * (s[n] + after(s, n)) for n in range(count)]
    s = [s[n] + LIFT_DELTA * (before(d, n) + d[n]) for n in range(count)]
    return [v * LIFT_SCALE for v in s], [v * LIFT_INVERSE for v in d]


def row_lift(s, d):
    rows = s.shape[0]
    after = lambda v: pltpu.roll(v, rows - 1, 0)
    before = lambda v: pltpu.roll(v, 1, 0)
    d = d + LIFT_ALPHA * (s + after(s))
    s = s + LIFT_BETA * (before(d) + d)
    d = d + LIFT_GAMMA * (s + after(s))
    s = s + LIFT_DELTA * (before(d) + d)
    return s * LIFT_SCALE, d * LIFT_INVERSE


def exchange_kernel(x_ref, z_ref, field, strips, load_sem, send_sem, recv_sem):
    nx, ny = lax.axis_size("gx"), lax.axis_size("gy")
    gx, gy = lax.axis_index("gx"), lax.axis_index("gy")
    up, down = lax.rem(gx + nx - 1, nx), lax.rem(gx + 1, nx)
    left, right = lax.rem(gy + ny - 1, ny), lax.rem(gy + 1, ny)
    barrier = pltpu.get_barrier_semaphore()
    around = [(up, gy), (down, gy), (gx, left), (gx, right), (up, left), (up, right), (down, left), (down, right)]
    for device in around:
        pl.semaphore_signal(barrier, inc=1, device_id=device, device_id_type=MESH)

    chunk = N // 4
    loads = []
    for c in range(4):
        rows = pl.ds(c * chunk, chunk)
        loads.append(pltpu.make_async_copy(x_ref.at[:, rows], field.at[:, rows], load_sem.at[c]))
        loads[-1].start()
    lane = lax.broadcasted_iota(jnp.int32, (8, N), 1)

    def block(i, _):
        at = pl.multiple_of(i * 8, 8)
        low, high = mirror_lift([field[z, pl.ds(at, 8), :] for z in range(16)])
        own = pl.ds(at + TOP, 8)
        for n in range(8):
            z_ref[n, own, :] = low[n]
            z_ref[HIGH + n, own, :] = high[n]
        here = pl.ds(at, 8)
        for g in range(3):
            group = [low[:4], low[4:], high][g]
            count = len(group)
            wide = N // count
            to_right, to_left = None, None
            for j in range(count):
                shift = wide * (j + 1) % N
                turned = pltpu.roll(group[j], shift, 1) if shift else group[j]
                slot = lane // wide
                to_right = turned if j == 0 else jnp.where(slot == j, turned, to_right)
                to_left = turned if j == 0 else jnp.where(slot == (j + 1) % count, turned, to_left)
            strips[g, here, :] = to_right
            strips[3 + g, here, :] = to_left
        return 0

    for c in range(4):
        loads[c].wait()
        lax.fori_loop(c * 4, c * 4 + 4, block, 0)

    pl.semaphore_wait(barrier, len(around))
    low, high = pl.ds(0, 8), pl.ds(HIGH, 8)
    lefts, rights = pl.ds(LEFT, 3), pl.ds(RIGHT, 3)
    to_right, to_left = pl.ds(0, 3), pl.ds(3, 3)
    own = pl.ds(TOP, N)
    head, tail = pl.ds(0, 24), pl.ds(N - 32, 32)
    above, below = pl.ds(0, 32), pl.ds(TOP + N, 24)
    moves = [
        (z_ref.at[low, pl.ds(TOP + N - 32, 32)], z_ref.at[low, above], (down, gy)),
        (z_ref.at[low, pl.ds(TOP, 24)], z_ref.at[low, below], (up, gy)),
        (z_ref.at[high, pl.ds(TOP + N - 8, 8)], z_ref.at[high, pl.ds(TOP - 8, 8)], (down, gy)),
        (z_ref.at[high, pl.ds(TOP, 8)], z_ref.at[high, pl.ds(TOP + N, 8)], (up, gy)),
        (strips.at[to_right], z_ref.at[lefts, own], (gx, right)),
        (strips.at[to_left], z_ref.at[rights, own], (gx, left)),
        (strips.at[to_right, tail], z_ref.at[lefts, above], (down, right)),
        (strips.at[to_right, head], z_ref.at[lefts, below], (up, right)),
        (strips.at[to_left, tail], z_ref.at[rights, above], (down, left)),
        (strips.at[to_left, head], z_ref.at[rights, below], (up, left)),
    ]
    copies = []
    for k, (source, target, device) in enumerate(moves):
        copies.append(
            pltpu.make_async_remote_copy(
                src_ref=source,
                dst_ref=target,
                send_sem=send_sem.at[k],
                recv_sem=recv_sem.at[k],
                device_id=device,
                device_id_type=MESH,
            )
        )
        copies[-1].start()
    for copy in copies:
        copy.wait_recv()
    for copy in copies:
        copy.wait_send()


def exchange(field):
    return pl.pallas_call(
        exchange_kernel,
        out_shape=jax.ShapeDtypeStruct((PLANES, EXT, N), jnp.float32),
        in_specs=[pl.BlockSpec(memory_space=pl.ANY)],
        out_specs=pl.BlockSpec(memory_space=pltpu.VMEM),
        scratch_shapes=[
            pltpu.VMEM((16, N, N), jnp.float32),
            pltpu.VMEM((6, N, N), jnp.float32),
            pltpu.SemaphoreType.DMA((4,)),
            pltpu.SemaphoreType.DMA((10,)),
            pltpu.SemaphoreType.DMA((10,)),
        ],
        compiler_params=pltpu.CompilerParams(collective_id=0, has_side_effects=True, vmem_limit_bytes=16 << 20),
        name="exchange",
    )(field)


def transform_kernel(z_ref, w_ref, one_ref, two_ref, three_ref, last_ref, r1, z2, r2, z3, r3, y2, y3):
    half, quarter, eighth = N // 2, N // 4, N // 8

    def first(p, _):
        s, d = row_lift(z_ref[p, pl.ds(0, EXT // 2, stride=2), :], z_ref[p, pl.ds(1, EXT // 2, stride=2), :])
        z2[p] = s
        r1[p, pl.ds(0, half), :] = s[TOP // 2 : TOP // 2 + half]
        r1[p, pl.ds(half, half), :] = d[TOP // 2 : TOP // 2 + half]
        return 0

    def later(p, _):
        s, d = row_lift(z2[p, pl.ds(0, EXT // 4, stride=2), :], z2[p, pl.ds(1, EXT // 4, stride=2), :])
        z3[p] = s
        r2[p, pl.ds(0, quarter), :] = s[TOP // 4 : TOP // 4 + quarter]
        r2[p, pl.ds(quarter, quarter), :] = d[TOP // 4 : TOP // 4 + quarter]
        s, d = row_lift(z3[p, pl.ds(0, EXT // 8, stride=2), :], z3[p, pl.ds(1, EXT // 8, stride=2), :])
        r3[p, pl.ds(0, eighth), :] = s[TOP // 8 : TOP // 8 + eighth]
        r3[p, pl.ds(eighth, eighth), :] = d[TOP // 8 : TOP // 8 + eighth]
        return 0

    lax.fori_loop(0, PLANES, first, 0)
    lax.fori_loop(0, DEEP, later, 0)

    def along_y(r, plane, group, slot, count, level):
        wide = N // count
        lane = lax.broadcasted_iota(jnp.int32, r.shape[1:], 1)
        halo = jnp.where(lane // wide == slot, r[LEFT + group], r[RIGHT + group])
        shift = lax.rem(2 * N - wide * (slot + 1), N)
        halo = pltpu.roll(halo, shift, 1)
        return jnp.dot(
            jnp.concatenate([r[plane], halo], axis=1),
            w_ref[level],
            precision=lax.Precision.HIGHEST,
            preferred_element_type=jnp.float32,
        )

    def low_planes(p, _):
        group, slot = p // 4, lax.rem(p, 4)
        out = along_y(r1, p, group, slot, 4, 0)
        one_ref[0, p] = out[half:, :half]
        one_ref[1, p] = out[:half, half:]
        one_ref[2, p] = out[half:, half:]
        y2[p] = along_y(r2, p, group, slot, 4, 1)
        y3[p] = along_y(r3, p, group, slot, 4, 2)
        return 0

    def high_planes(q, _):
        out = along_y(r1, HIGH + q, 2, q, 8, 0)
        one_ref[3, q] = out[:half, :half]
        one_ref[4, q] = out[half:, :half]
        one_ref[5, q] = out[:half, half:]
        one_ref[6, q] = out[half:, half:]
        return 0

    lax.fori_loop(0, 8, low_planes, 0)
    lax.fori_loop(0, 8, high_planes, 0)

    def put(ref, last, low, high, size):
        for n in range(len(low)):
            for band, planes in ((0, low), (4, high)):
                v = planes[n]
                for j in range(4):
                    by, bx = j // 2, j % 2
                    part = v[bx * size : (bx + 1) * size, by * size : (by + 1) * size]
                    if band + j:
                        ref[band + j - 1, n] = part
                    elif last is not None:
                        last[n] = part

    low, high = mirror_lift([y2[p] for p in range(8)])
    put(two_ref, None, low, high, quarter)
    low, _ = mirror_lift([y3[p] for p in range(8)])
    low, high = mirror_lift(low)
    put(three_ref, last_ref, low, high, eighth)


def transform(extended, filters):
    f32 = jnp.float32
    vmem = pl.BlockSpec(memory_space=pltpu.VMEM)
    return pl.pallas_call(
        transform_kernel,
        out_shape=(
            jax.ShapeDtypeStruct((7, 8, N // 2, N // 2), f32),
            jax.ShapeDtypeStruct((7, 4, N // 4, N // 4), f32),
            jax.ShapeDtypeStruct((7, 2, N // 8, N // 8), f32),
            jax.ShapeDtypeStruct((2, N // 8, N // 8), f32),
        ),
        in_specs=[vmem, vmem],
        out_specs=(vmem,) * 4,
        scratch_shapes=[
            pltpu.VMEM((PLANES, N, N), f32),
            pltpu.VMEM((PLANES, EXT // 2, N), f32),
            pltpu.VMEM((DEEP, N // 2, N), f32),
            pltpu.VMEM((DEEP, EXT // 4, N), f32),
            pltpu.VMEM((DEEP, N // 4, N), f32),
            pltpu.VMEM((8, N // 2, N), f32),
            pltpu.VMEM((8, N // 4, N), f32),
        ],
        compiler_params=pltpu.CompilerParams(vmem_limit_bytes=24 << 20),
        name="transform",
    )(extended, filters)


def shards(ocean_field):
    return transform(exchange(ocean_field), jnp.asarray(lane_filters()))


def solution(mesh):
    return jax.shard_map(
        shards,
        mesh=mesh,
        in_specs=(P(None, "gx", "gy"),),
        out_specs=(
            P(None, None, "gx", "gy"),
            P(None, None, "gx", "gy"),
            P(None, None, "gx", "gy"),
            P(None, "gx", "gy"),
        ),
        check_vma=False,
    )
```

time: 135 us -> 28.3 us (0.21)
  the two profiles are of different devices: /device:TPU:94 before, /device:TPU:1 now
where the time goes in v1:
time: 28.3 us; the launch traced here: 28.1 us
  Pallas kernels  26.3 us (93%)
  local copies, waits for them, and re-layouts  1.22 us (4%)
  between operations  0.65 us (2%)
    pallas_call x1, Pallas kernels, exchange(): pl.pallas_call(exchange_kernel, out_shape=jax.ShapeDtypeStruct((PLANES, E...  16.6 us
    pallas_call x1, Pallas kernels, transform(): pl.pallas_call(transform_kernel, out_shape=(jax.ShapeDtypeStruct((7, 8, N...  9.64 us
    unnamed x4, local copies, waits for them, and re-layouts  1.22 us

profile of v1, /device:TPU:1, one launch (start us, length us, event | category | flops | bytes accessed | tf_op | source)
XLA Modules:
  0.0 28.1 jit_solution(9964454488817513268)
XLA Ops:
  0.6 0.0 copy-start
  0.6 1.2 %copy-done = f32[16,128,128]{2,1,0:T(8,128)S(1)} copy-done((f32[16,128,128]{2,1,0:T(8,128)S(1)}, f32[16,128,128]{2,1,0:T(8,128)}, u32[]{:S(2)}) %copy-start) | copy-done | bytes 1048600
  1.9 0.0 copy-start.1
  1.9 16.6 %exchange.1.z_ref = f32[22,192,128]{2,1,0:T(8,128)S(1)} custom-call(f32[16,128,128]{2,1,0:T(8,128)S(1)} %copy-done), custom_call_target="tpu_custom_call" | custom-call | tf_op jit(solution)/shard_map/exchange/pallas_call | solution.py:154
  18.5 0.0 copy-done.1
  18.5 9.6 %transform.1 = (f32[7,8,64,64]{3,2,1,0:T(8,128)}, f32[7,4,32,32]{3,2,1,0:T(8,128)}, f32[7,2,16,16]{3,2,1,0:T(8,128)}, f32[2,16,16]{2,1,0:T(8,128)}) custom-call(f32[22,192,128]{2,1,0:T(8,128)S(1)} %exchange.1.z_ref, f32[3,256,128]{2,1,0:T(8,128)S(1)} %copy-done.1), custom_call_target="tpu_custom_call" | custom-call | tf_op jit(solution)/shard_map/transform/pallas_call | solution.py:250
Async XLA Ops:
  0.6 1.2 %copy-start = (f32[16,128,128]{2,1,0:T(8,128)S(1)}, f32[16,128,128]{2,1,0:T(8,128)}, u32[]{:S(2)}) copy-start(f32[16,128,128]{2,1,0:T(8,128)} %x_ref.1) | copy-start | bytes 3145732
  1.9 16.6 %copy-start.1 = (f32[3,256,128]{2,1,0:T(8,128)S(1)}, f32[3,256,128]{2,1,0:T(8,128)}, u32[]{:S(2)}) copy-start(f32[3,256,128]{2,1,0:T(8,128)} %constant.2.clone.w_ref) | copy-start | bytes 1179652

commit v2 on v1

--- a/solution.py
+++ b/solution.py
@@ -2,6 +2,7 @@
 
 import jax
 import jax.numpy as jnp
+import ml_dtypes
 import numpy as np
 from jax import lax
 from jax.experimental import pallas as pl
@@ -20,7 +21,9 @@
 TOP = 32
 EXT = 192
 LEFT, RIGHT, HIGH, PLANES = 8, 11, 14, 22
-DEEP = 13
+OWN, OWN_DEEP, HALO_DEEP, STRIPS = 0, 1, 2, 3
+PAD = 16
+DEEP = [0, 1, 2, 3, 4, 5, 6, 7, 8, 9, 11, 12]
 
 
 def lift_matrix(extent):
@@ -40,8 +43,42 @@
     one = np.concatenate([low1[: N // 2], high1[: N // 2]]).T
     two = np.concatenate([(low2 @ low1)[: N // 4], (high2 @ low1)[: N // 4]]).T
     three = np.concatenate([(low3 @ low2 @ low1)[: N // 8], (high3 @ low2 @ low1)[: N // 8]]).T
-    pad = lambda w: np.pad(w, ((0, 0), (0, N - w.shape[1]))).astype(np.float32)
-    return np.stack([pad(one), pad(two), pad(three)])
+    return one, np.concatenate([two, three, np.zeros((2 * N, N // 4))], axis=1)
+
+
+def strip_filters(one):
+    out = np.zeros((6, N, N))
+    for plane in range(16):
+        group, count = (plane // 4, 4) if plane < 8 else (2, 8)
+        slot, wide = plane % count, N // count
+        for near in range(wide):
+            for k, column in enumerate((126, 127, 0, 1)):
+                out[group, slot * wide + near, 4 * plane + k] = one[2 * N - wide + near, column]
+                out[3 + group, (slot + 1) % count * wide + near, 4 * plane + k] = one[N + near, column]
+            for k, column in enumerate((62, 63, 64)):
+                out[group, slot * wide + near, 64 + 4 * plane + k] = one[2 * N - wide + near, column]
+                out[3 + group, (slot + 1) % count * wide + near, 64 + 4 * plane + k] = one[N + near, column]
+    return out
+
+
+def parts(values, kind):
+    high = values.astype(kind)
+    rest = values - high.astype(values.dtype)
+    middle = rest.astype(kind)
+    return high, middle, (rest - middle.astype(values.dtype)).astype(kind)
+
+
+def paired(weights):
+    high, middle, low = parts(weights, ml_dtypes.bfloat16)
+    first = np.concatenate([np.concatenate([high, middle], -1), np.concatenate([middle, high], -1)], -2)
+    return first, np.concatenate([low, high], -2)
+
+
+def product(values, first, second):
+    high, middle, low = parts(values, jnp.bfloat16)
+    wide = jnp.dot(jnp.concatenate([high, middle], axis=1), first, preferred_element_type=jnp.float32)
+    rest = jnp.dot(jnp.concatenate([high, low], axis=1), second, preferred_element_type=jnp.float32)
+    return wide[:, :N] + (wide[:, N:] + rest)
 
 
 def mirror_lift(planes):
@@ -67,7 +104,9 @@
     return s * LIFT_SCALE, d * LIFT_INVERSE
 
 
-def exchange_kernel(x_ref, z_ref, field, strips, load_sem, send_sem, recv_sem):
+def exchange_kernel(
+    x_ref, first_ref, second_ref, z_ref, own_ref, first, second, field, strips, padded, load_sem, send_sem, recv_sem
+):
     nx, ny = lax.axis_size("gx"), lax.axis_size("gy")
     gx, gy = lax.axis_index("gx"), lax.axis_index("gy")
     up, down = lax.rem(gx + nx - 1, nx), lax.rem(gx + 1, nx)
@@ -83,6 +122,12 @@
         rows = pl.ds(c * chunk, chunk)
         loads.append(pltpu.make_async_copy(x_ref.at[:, rows], field.at[:, rows], load_sem.at[c]))
         loads[-1].start()
+    weights = [
+        pltpu.make_async_copy(first_ref, first, load_sem.at[4]),
+        pltpu.make_async_copy(second_ref, second, load_sem.at[5]),
+    ]
+    for copy in weights:
+        copy.start()
     lane = lax.broadcasted_iota(jnp.int32, (8, N), 1)
 
     def block(i, _):
@@ -92,6 +137,8 @@
         for n in range(8):
             z_ref[n, own, :] = low[n]
             z_ref[HIGH + n, own, :] = high[n]
+            padded[n, pl.ds(at + PAD, 8), :] = low[n]
+            padded[8 + n, pl.ds(at + PAD, 8), :] = high[n]
         here = pl.ds(at, 8)
         for g in range(3):
             group = [low[:4], low[4:], high][g]
@@ -144,86 +191,146 @@
             )
         )
         copies[-1].start()
+
+    for copy in weights:
+        copy.wait()
+    padded[:, pl.ds(0, PAD), :] = jnp.zeros((16, PAD, N), jnp.float32)
+    padded[:, pl.ds(PAD + N, PAD), :] = jnp.zeros((16, PAD, N), jnp.float32)
+
+    def plane(p, _):
+        s, d = row_lift(
+            padded[p, pl.ds(0, PAD + N // 2, stride=2), :], padded[p, pl.ds(1, PAD + N // 2, stride=2), :]
+        )
+        rows = jnp.concatenate([s[PAD // 2 : PAD // 2 + N // 2], d[PAD // 2 : PAD // 2 + N // 2]])
+        own_ref[p] = product(rows, first[0], second[0])
+        return 0
+
+    lax.fori_loop(0, 16, plane, 0)
     for copy in copies:
         copy.wait_recv()
     for copy in copies:
         copy.wait_send()
 
 
-def exchange(field):
+def exchange(field, first, second):
+    f32 = jnp.float32
     return pl.pallas_call(
         exchange_kernel,
-        out_shape=jax.ShapeDtypeStruct((PLANES, EXT, N), jnp.float32),
-        in_specs=[pl.BlockSpec(memory_space=pl.ANY)],
-        out_specs=pl.BlockSpec(memory_space=pltpu.VMEM),
+        out_shape=(
+            jax.ShapeDtypeStruct((PLANES, EXT, N), f32),
+            jax.ShapeDtypeStruct((16, N, N), f32),
+            jax.ShapeDtypeStruct(first.shape, first.dtype),
+            jax.ShapeDtypeStruct(second.shape, second.dtype),
+        ),
+        in_specs=[pl.BlockSpec(memory_space=pltpu.HBM)] * 3,
+        out_specs=(pl.BlockSpec(memory_space=pltpu.VMEM),) * 4,
         scratch_shapes=[
-            pltpu.VMEM((16, N, N), jnp.float32),
-            pltpu.VMEM((6, N, N), jnp.float32),
-            pltpu.SemaphoreType.DMA((4,)),
+            pltpu.VMEM((16, N, N), f32),
+            pltpu.VMEM((6, N, N), f32),
+            pltpu.VMEM((16, N + 2 * PAD, N), f32),
+            pltpu.SemaphoreType.DMA((6,)),
             pltpu.SemaphoreType.DMA((10,)),
             pltpu.SemaphoreType.DMA((10,)),
         ],
-        compiler_params=pltpu.CompilerParams(collective_id=0, has_side_effects=True, vmem_limit_bytes=16 << 20),
+        compiler_params=pltpu.CompilerParams(collective_id=0, has_side_effects=True, vmem_limit_bytes=20 << 20),
         name="exchange",
-    )(field)
-
-
-def transform_kernel(z_ref, w_ref, one_ref, two_ref, three_ref, last_ref, r1, z2, r2, z3, r3, y2, y3):
+    )(*[pltpu.with_memory_space_constraint(v, pltpu.HBM) for v in (field, first, second)])
+
+
+def transform_kernel(
+    z_ref, own_ref, first, second,
+    one_ref, two_ref, three_ref, last_ref, one, two, three, last, edge, fix, z2, z3, strip, deep, sem,
+):
     half, quarter, eighth = N // 2, N // 4, N // 8
-
-    def first(p, _):
+    sub = lax.broadcasted_iota(jnp.int32, (8, N), 0)
+    lane = lax.broadcasted_iota(jnp.int32, (8, N), 1)
+    zero = jnp.zeros((8, N), jnp.float32)
+
+    for p in range(16):
+        q = p if p < 8 else HIGH + p - 8
+        edge[0, pl.ds(16 * p, 8), :] = z_ref[q, pl.ds(TOP - 8, 8), :]
+        edge[0, pl.ds(16 * p + 8, 8), :] = zero
+        edge[1, pl.ds(16 * p, 8), :] = zero
+        edge[1, pl.ds(16 * p + 8, 8), :] = z_ref[q, pl.ds(TOP + N, 8), :]
+    rows = []
+    for t, shift in ((0, N - 4), (1, 4)):
+        pair = row_lift(edge[t, pl.ds(0, N, stride=2), :], edge[t, pl.ds(1, N, stride=2), :])
+        rows.append([pltpu.roll(v, shift, 0) for v in pair])
+    place = lax.rem(lax.broadcasted_iota(jnp.int32, (N, N), 0), 8)
+    for bx in range(2):
+        both = jnp.where(place < 2 - bx, rows[0][bx], jnp.where(place >= 6, rows[1][bx], 0.0))
+        fix[bx] = product(both, first[OWN], second[OWN])
+
+    for p in range(14):
         s, d = row_lift(z_ref[p, pl.ds(0, EXT // 2, stride=2), :], z_ref[p, pl.ds(1, EXT // 2, stride=2), :])
-        z2[p] = s
-        r1[p, pl.ds(0, half), :] = s[TOP // 2 : TOP // 2 + half]
-        r1[p, pl.ds(half, half), :] = d[TOP // 2 : TOP // 2 + half]
+        if p in DEEP:
+            z2[p] = s
+        if p >= LEFT:
+            strip[p - LEFT, pl.ds(0, half), :] = s[TOP // 2 : TOP // 2 + half]
+            strip[p - LEFT, pl.ds(half, half), :] = d[TOP // 2 : TOP // 2 + half]
+    total = product(strip[0], first[STRIPS], second[STRIPS])
+    for t in range(1, 6):
+        total = total + product(strip[t], first[STRIPS + t], second[STRIPS + t])
+    strip[0] = total
+
+    reached = (lane < 2) | (lane >= N - 2) | ((lane >= half - 2) & (lane <= half))
+
+    def level_one(p, n, bands):
+        across = pltpu.roll(strip[0], lax.rem(2 * N - 2 - 4 * p, N), 1)
+        for bx in range(2):
+            extra = fix[bx, pl.ds(pl.multiple_of(8 * p, 8), 8), :]
+            for r in range(8):
+                at = half * bx + 8 * r
+                v = own_ref[p, pl.ds(at, 8), :] + jnp.where(reached, across[at : at + 8], zero)
+                if r == 0:
+                    v = v + jnp.where(sub < 4, extra, zero)
+                elif r == 7:
+                    v = v + jnp.where(sub >= 4, extra, zero)
+                if bands[bx] is not None:
+                    one[bands[bx], n, pl.ds(8 * r, 8), :] = v[:, :half]
+                one[bands[2 + bx], n, pl.ds(8 * r, 8), :] = pltpu.roll(v, half, 1)[:, :half]
+
+    def low_plane(p, _):
+        level_one(p, p, (None, 0, 1, 2))
         return 0
 
-    def later(p, _):
+    def high_plane(p, _):
+        level_one(p, p - 8, (3, 4, 5, 6))
+        return 0
+
+    outs = [
+        pltpu.make_async_copy(one.at[pl.ds(0, 3)], one_ref.at[pl.ds(0, 3)], sem.at[0]),
+        pltpu.make_async_copy(one.at[pl.ds(3, 4)], one_ref.at[pl.ds(3, 4)], sem.at[1]),
+        pltpu.make_async_copy(two, two_ref, sem.at[2]),
+        pltpu.make_async_copy(three, three_ref, sem.at[3]),
+        pltpu.make_async_copy(last, last_ref, sem.at[4]),
+    ]
+    lax.fori_loop(8, 16, high_plane, 0)
+    outs[1].start()
+    lax.fori_loop(0, 8, low_plane, 0)
+    outs[0].start()
+
+    for p in DEEP:
         s, d = row_lift(z2[p, pl.ds(0, EXT // 4, stride=2), :], z2[p, pl.ds(1, EXT // 4, stride=2), :])
         z3[p] = s
-        r2[p, pl.ds(0, quarter), :] = s[TOP // 4 : TOP // 4 + quarter]
-        r2[p, pl.ds(quarter, quarter), :] = d[TOP // 4 : TOP // 4 + quarter]
+        deep[p, pl.ds(0, quarter), :] = s[TOP // 4 : TOP // 4 + quarter]
+        deep[p, pl.ds(quarter, quarter), :] = d[TOP // 4 : TOP // 4 + quarter]
+    for p in DEEP:
         s, d = row_lift(z3[p, pl.ds(0, EXT // 8, stride=2), :], z3[p, pl.ds(1, EXT // 8, stride=2), :])
-        r3[p, pl.ds(0, eighth), :] = s[TOP // 8 : TOP // 8 + eighth]
-        r3[p, pl.ds(eighth, eighth), :] = d[TOP // 8 : TOP // 8 + eighth]
-        return 0
-
-    lax.fori_loop(0, PLANES, first, 0)
-    lax.fori_loop(0, DEEP, later, 0)
-
-    def along_y(r, plane, group, slot, count, level):
-        wide = N // count
-        lane = lax.broadcasted_iota(jnp.int32, r.shape[1:], 1)
-        halo = jnp.where(lane // wide == slot, r[LEFT + group], r[RIGHT + group])
-        shift = lax.rem(2 * N - wide * (slot + 1), N)
-        halo = pltpu.roll(halo, shift, 1)
-        return jnp.dot(
-            jnp.concatenate([r[plane], halo], axis=1),
-            w_ref[level],
-            precision=lax.Precision.HIGHEST,
-            preferred_element_type=jnp.float32,
-        )
-
-    def low_planes(p, _):
-        group, slot = p // 4, lax.rem(p, 4)
-        out = along_y(r1, p, group, slot, 4, 0)
-        one_ref[0, p] = out[half:, :half]
-        one_ref[1, p] = out[:half, half:]
-        one_ref[2, p] = out[half:, half:]
-        y2[p] = along_y(r2, p, group, slot, 4, 1)
-        y3[p] = along_y(r3, p, group, slot, 4, 2)
-        return 0
-
-    def high_planes(q, _):
-        out = along_y(r1, HIGH + q, 2, q, 8, 0)
-        one_ref[3, q] = out[:half, :half]
-        one_ref[4, q] = out[half:, :half]
-        one_ref[5, q] = out[:half, half:]
-        one_ref[6, q] = out[half:, half:]
-        return 0
-
-    lax.fori_loop(0, 8, low_planes, 0)
-    lax.fori_loop(0, 8, high_planes, 0)
+        deep[p, pl.ds(half, eighth), :] = s[TOP // 8 : TOP // 8 + eighth]
+        deep[p, pl.ds(half + eighth, eighth), :] = d[TOP // 8 : TOP // 8 + eighth]
+    depth = half + quarter
+    slots = lax.broadcasted_iota(jnp.int32, (depth, N), 1) // 32
+    halo = []
+    for p in range(8):
+        group, slot = p // 4, p % 4
+        v = jnp.where(slots == slot, deep[LEFT + group], deep[RIGHT + group])
+        halo.append(pltpu.roll(v, N - 32 * (slot + 1), 1) if slot < 3 else v)
+    own = jnp.concatenate([deep[p] for p in range(8)])
+    out = product(own, first[OWN_DEEP], second[OWN_DEEP]) + product(
+        jnp.concatenate(halo), first[HALO_DEEP], second[HALO_DEEP]
+    )
+    out = out.reshape(8, depth, N)
 
     def put(ref, last, low, high, size):
         for n in range(len(low)):
@@ -237,42 +344,51 @@
                     elif last is not None:
                         last[n] = part
 
-    low, high = mirror_lift([y2[p] for p in range(8)])
-    put(two_ref, None, low, high, quarter)
-    low, _ = mirror_lift([y3[p] for p in range(8)])
+    low, high = mirror_lift([out[p, :half, :half] for p in range(8)])
+    put(two, None, low, high, quarter)
+    outs[2].start()
+    low, _ = mirror_lift([out[p, half:, half:depth] for p in range(8)])
     low, high = mirror_lift(low)
-    put(three_ref, last_ref, low, high, eighth)
-
-
-def transform(extended, filters):
+    put(three, last, low, high, eighth)
+    outs[3].start()
+    outs[4].start()
+    for copy in outs:
+        copy.wait()
+
+
+def transform(extended, own, first, second):
     f32 = jnp.float32
     vmem = pl.BlockSpec(memory_space=pltpu.VMEM)
+    shapes = (
+        (7, 8, N // 2, N // 2),
+        (7, 4, N // 4, N // 4),
+        (7, 2, N // 8, N // 8),
+        (2, N // 8, N // 8),
+    )
     return pl.pallas_call(
         transform_kernel,
-        out_shape=(
-            jax.ShapeDtypeStruct((7, 8, N // 2, N // 2), f32),
-            jax.ShapeDtypeStruct((7, 4, N // 4, N // 4), f32),
-            jax.ShapeDtypeStruct((7, 2, N // 8, N // 8), f32),
-            jax.ShapeDtypeStruct((2, N // 8, N // 8), f32),
-        ),
-        in_specs=[vmem, vmem],
-        out_specs=(vmem,) * 4,
-        scratch_shapes=[
-            pltpu.VMEM((PLANES, N, N), f32),
-            pltpu.VMEM((PLANES, EXT // 2, N), f32),
-            pltpu.VMEM((DEEP, N // 2, N), f32),
-            pltpu.VMEM((DEEP, EXT // 4, N), f32),
-            pltpu.VMEM((DEEP, N // 4, N), f32),
-            pltpu.VMEM((8, N // 2, N), f32),
-            pltpu.VMEM((8, N // 4, N), f32),
+        out_shape=tuple(jax.ShapeDtypeStruct(shape, f32) for shape in shapes),
+        in_specs=[vmem] * 4,
+        out_specs=(pl.BlockSpec(memory_space=pltpu.HBM),) * 4,
+        scratch_shapes=[pltpu.VMEM(shape, f32) for shape in shapes]
+        + [
+            pltpu.VMEM((2, 2 * N, N), f32),
+            pltpu.VMEM((2, N, N), f32),
+            pltpu.VMEM((14, EXT // 2, N), f32),
+            pltpu.VMEM((14, EXT // 4, N), f32),
+            pltpu.VMEM((6, N, N), f32),
+            pltpu.VMEM((14, N // 2 + N // 4, N), f32),
+            pltpu.SemaphoreType.DMA((5,)),
         ],
         compiler_params=pltpu.CompilerParams(vmem_limit_bytes=24 << 20),
         name="transform",
-    )(extended, filters)
+    )(extended, own, first, second)
 
 
 def shards(ocean_field):
-    return transform(exchange(ocean_field), jnp.asarray(lane_filters()))
+    one, deep = lane_filters()
+    first, second = paired(np.concatenate([one[None, :N], deep[None, :N], deep[None, N:], strip_filters(one)]))
+    return transform(*exchange(ocean_field, jnp.asarray(first), jnp.asarray(second)))
 
 
 def solution(mesh):

time: 28.3 us -> 23 us (0.81)
  Pallas kernels: 26.3 us -> 22.3 us
  local copies, waits for them, and re-layouts: 1.22 us -> 0 us
    pallas_call x2, Pallas kernels: 26.3 us -> 22.3 us  [the longest x1 16.7 us: exchange(): pl.pallas_call(exchange_kernel, out_shape=(jax.ShapeDtypeStruct((PLANES,...]
    unnamed x4 -> x0, local copies, waits for them, and re-layouts: 1.22 us -> none
where the time goes in v2:
time: 23 us; the launch traced here: 22.9 us
  Pallas kernels  22.3 us (97%)
  between operations  0.64 us (3%)
    pallas_call x1, Pallas kernels, exchange(): pl.pallas_call(exchange_kernel, out_shape=(jax.ShapeDtypeStruct((PLANES,...  16.7 us
    pallas_call x1, Pallas kernels, transform(): pl.pallas_call(transform_kernel, out_shape=tuple((jax.ShapeDtypeStruct(sh...  5.58 us

profile of v2, /device:TPU:1, one launch (start us, length us, event | category | flops | bytes accessed | tf_op | source)
XLA Modules:
  0.0 22.9 jit_solution(8874669032492542574)
XLA Ops:
  0.6 16.7 %exchange.1 = (f32[22,192,128]{2,1,0:T(8,128)S(1)}, f32[16,128,128]{2,1,0:T(8,128)S(1)}, bf16[9,256,256]{2,1,0:T(8,128)(2,1)S(1)}, bf16[9,256,128]{2,1,0:T(8,128)(2,1)S(1)}) custom-call(f32[16,128,128]{2,1,0:T(8,128)} %x_ref.1, bf16[9,256,256]{2,1,0:T(8,128)(2,1)} %constant.4.clone.first_ref, bf16[9,256,128]{2,1,0:T(8,128)(2,1)} %constant.5.clone.second_ref), custom_call_target="tpu_custom_call" | custom-call | tf_op jit(solution)/shard_map/exchange/pallas_call | solution.py:217
  17.3 5.6 %transform.1 = (f32[7,8,64,64]{3,2,1,0:T(8,128)}, f32[7,4,32,32]{3,2,1,0:T(8,128)}, f32[7,2,16,16]{3,2,1,0:T(8,128)}, f32[2,16,16]{2,1,0:T(8,128)}) custom-call(f32[22,192,128]{2,1,0:T(8,128)S(1)} %get-tuple-element.8.z_ref, f32[16,128,128]{2,1,0:T(8,128)S(1)} %get-tuple-element.9.own_ref, bf16[9,256,256]{2,1,0:T(8,128)(2,1)S(1)} %get-tuple-element.10.first, ...), custom_call_target="tpu_custom_call" | custom-call | tf_op jit(solution)/shard_map/transform/pallas_call | solution.py:368

commit v3 on v2

v3 whole, which is shorter than its diff:
```python
import functools

import jax
import jax.numpy as jnp
import ml_dtypes
import numpy as np
from jax import lax
from jax.experimental import pallas as pl
from jax.experimental.pallas import tpu as pltpu
from jax.sharding import PartitionSpec as P

LIFT_ALPHA = -1.586134342
LIFT_BETA = -0.05298011854
LIFT_GAMMA = 0.8829110762
LIFT_DELTA = 0.4435068522
LIFT_SCALE = 1.149604398
LIFT_INVERSE = 0.869864452

MESH = pl.DeviceIdType.MESH
N = 128
HALF, QUARTER, EIGHTH = N // 2, N // 4, N // 8
PAD = 32
ROWS = N + HALF + QUARTER
SPILL = 24
BLOCKS = 160
OWN, OWN_DEEP, REACH = 0, 1, 2
HIGH2, LOW3, HIGH3 = 40, 96, 112


def lift_matrix(extent):
    v = np.eye(extent)
    s, d = v[0::2], v[1::2]
    d = d + LIFT_ALPHA * (s + np.roll(s, -1, 0))
    s = s + LIFT_BETA * (np.roll(d, 1, 0) + d)
    d = d + LIFT_GAMMA * (s + np.roll(s, -1, 0))
    s = s + LIFT_DELTA * (np.roll(d, 1, 0) + d)
    return LIFT_SCALE * s, LIFT_INVERSE * d


def lane_filters():
    low1, high1 = lift_matrix(2 * N)
    low2, high2 = lift_matrix(N)
    low3, high3 = lift_matrix(HALF)
    one = np.concatenate([low1[:HALF], high1[:HALF]]).T
    deep = np.zeros((2 * N, N))
    deep[:, :QUARTER] = (low2 @ low1)[:QUARTER].T
    deep[:, HIGH2 : HIGH2 + QUARTER] = (high2 @ low1)[:QUARTER].T
    deep[:, LOW3:HIGH3] = (low3 @ low2 @ low1)[:EIGHTH].T
    deep[:, HIGH3:] = (high3 @ low2 @ low1)[:EIGHTH].T
    reach = np.zeros((6, N, N))
    for level, (filters, count, stride, columns) in enumerate(
        (
            (one, 16, 4, (0, 1, 62, 63, 64, 126, 127)),
            (deep, 8, 16, columns_two()),
            (deep, 4, 32, columns_three()),
        )
    ):
        wide = N // count
        for p in range(count):
            after = (p + 1) % count
            for column in columns:
                to = (column + stride * p + (2 if level == 0 else 0)) % N
                reach[2 * level, p * wide : (p + 1) * wide, to] = filters[2 * N - wide :, column]
                reach[2 * level + 1, after * wide : (after + 1) * wide, to] = filters[N : N + wide, column]
    return np.concatenate([one[None, :N], deep[None, :N], reach])


def columns_two():
    return (0, 1, 2, 29, 30, 31) + tuple(HIGH2 + c for c in (0, 1, 29, 30, 31))


def columns_three():
    return tuple(LOW3 + c for c in (0, 1, 2, 3, 13, 14, 15, 16, 17, 18, 29, 30, 31))


def parts(values, kind):
    high = values.astype(kind)
    rest = values - high.astype(values.dtype)
    middle = rest.astype(kind)
    return high, middle, (rest - middle.astype(values.dtype)).astype(kind)


def paired(weights):
    high, middle, low = parts(weights, ml_dtypes.bfloat16)
    first = np.concatenate([np.concatenate([high, middle], -1), np.concatenate([middle, high], -1)], -2)
    return first, np.concatenate([low, high], -2)


def product(values, first, second):
    high, middle, low = parts(values, jnp.bfloat16)
    wide = jnp.dot(jnp.concatenate([high, middle], axis=1), first, preferred_element_type=jnp.float32)
    rest = jnp.dot(jnp.concatenate([high, low], axis=1), second, preferred_element_type=jnp.float32)
    return wide[:, :N] + (wide[:, N:] + rest)


def mirror_lift(planes):
    count = len(planes) // 2
    s, d = list(planes[0::2]), list(planes[1::2])
    after = lambda v, n: v[min(n + 1, count - 1)]
    before = lambda v, n: v[max(n - 1, 0)]
    d = [d[n] + LIFT_ALPHA * (s[n] + after(s, n)) for n in range(count)]
    s = [s[n] + LIFT_BETA * (before(d, n) + d[n]) for n in range(count)]
    d = [d[n] + LIFT_GAMMA * (s[n] + after(s, n)) for n in range(count)]
    s = [s[n] + LIFT_DELTA * (before(d, n) + d[n]) for n in range(count)]
    return [v * LIFT_SCALE for v in s], [v * LIFT_INVERSE for v in d]


def row_lift(s, d):
    rows = s.shape[0]
    after = lambda v: pltpu.roll(v, rows - 1, 0)
    before = lambda v: pltpu.roll(v, 1, 0)
    d = d + LIFT_ALPHA * (s + after(s))
    s = s + LIFT_BETA * (before(d) + d)
    d = d + LIFT_GAMMA * (s + after(s))
    s = s + LIFT_DELTA * (before(d) + d)
    return s * LIFT_SCALE, d * LIFT_INVERSE


def exchange_kernel(
    x_ref, first_ref, second_ref, own1, own2, own3, xr, yr, first, second,
    field, padded, r1, r2, r3, z2, z3, xs, ys, load_sem, send_sem, recv_sem,
):
    nx, ny = lax.axis_size("gx"), lax.axis_size("gy")
    gx, gy = lax.axis_index("gx"), lax.axis_index("gy")
    up, down = lax.rem(gx + nx - 1, nx), lax.rem(gx + 1, nx)
    left, right = lax.rem(gy + ny - 1, ny), lax.rem(gy + 1, ny)
    barrier = pltpu.get_barrier_semaphore()
    around = [(up, gy), (down, gy), (gx, left), (gx, right), (up, left), (up, right), (down, left), (down, right)]
    for device in around:
        pl.semaphore_signal(barrier, inc=1, device_id=device, device_id_type=MESH)

    chunk = N // 4
    loads = []
    for c in range(4):
        rows = pl.ds(c * chunk, chunk)
        loads.append(pltpu.make_async_copy(x_ref.at[:, rows], field.at[:, rows], load_sem.at[c]))
        loads[-1].start()
    weights = [
        pltpu.make_async_copy(first_ref, first, load_sem.at[4]),
        pltpu.make_async_copy(second_ref, second, load_sem.at[5]),
    ]
    for copy in weights:
        copy.start()

    edge = jnp.zeros((16, PAD, N), jnp.float32)
    padded[:, pl.ds(0, PAD), :] = edge
    padded[:, pl.ds(PAD + N, PAD), :] = edge
    for array, rows, edges in ((z2, HALF + 64, 24), (z3, QUARTER + 32, 8)):
        edge = jnp.zeros((array.shape[0], edges, N), jnp.float32)
        array[:, pl.ds(0, edges), :] = edge
        array[:, pl.ds(rows - edges, edges), :] = edge

    def depth(i, _):
        at = pl.multiple_of(i * 8, 8)
        low, high = mirror_lift([field[z, pl.ds(at, 8), :] for z in range(16)])
        for n in range(8):
            padded[n, pl.ds(at + PAD, 8), :] = low[n]
            padded[8 + n, pl.ds(at + PAD, 8), :] = high[n]
        return 0

    for c in range(4):
        loads[c].wait()
        lax.fori_loop(c * 4, c * 4 + 4, depth, 0, unroll=2)

    def spills(s, d, begin, end, shift_up, shift_down):
        over = s[begin - 8 : begin] + pltpu.roll(d[begin - 8 : begin], 8 - shift_up, 0)
        under = s[end : end + 8] + pltpu.roll(d[end : end + 8], shift_down, 0)
        return over, under

    def rows_one(p, _):
        both = []
        for q in (p, p + 8):
            s, d = row_lift(padded[q, pl.ds(0, 96, stride=2), :], padded[q, pl.ds(1, 96, stride=2), :])
            r1[q, pl.ds(0, HALF), :] = s[16 : 16 + HALF]
            r1[q, pl.ds(HALF, HALF), :] = d[16 : 16 + HALF]
            over, under = spills(s, d, 16, 80, 2, 2)
            r1[q, pl.ds(N, 8), :] = over
            r1[q, pl.ds(N + 8, 8), :] = under
            both.append((over, under))
            if q is p:
                z2[p, pl.ds(24, 80), :] = s[8:88]
        at = pl.ds(pl.multiple_of(8 * p, 8), 8)
        for way in range(2):
            xs[way, at, :] = both[0][way] + pltpu.roll(both[1][way], 4, 0)
        return 0

    lax.fori_loop(0, 8, rows_one, 0)

    def depth_two(i, _):
        at = pl.ds(pl.multiple_of(24 + 8 * i, 8), 8)
        low, high = mirror_lift([z2[p, at, :] for p in range(8)])
        for n in range(4):
            z2[n, at, :] = low[n]
            z2[4 + n, at, :] = high[n]
        return 0

    lax.fori_loop(0, 10, depth_two, 0, unroll=2)
    for p in range(8):
        s, d = row_lift(z2[p, pl.ds(0, 64, stride=2), :], z2[p, pl.ds(1, 64, stride=2), :])
        r2[p, pl.ds(0, QUARTER), :] = s[16 : 16 + QUARTER]
        r2[p, pl.ds(QUARTER, QUARTER), :] = d[16 : 16 + QUARTER]
        for way, part in enumerate(spills(s, d, 16, 48, 3, 3)):
            r2[p, pl.ds(HALF + 8 * way, 8), :] = part
            xs[way, pl.ds(HALF + 8 * p, 8), :] = part
        if p < 4:
            z3[p, pl.ds(8, 48), :] = s[8:56]
    for i in range(6):
        at = pl.ds(8 + 8 * i, 8)
        low, high = mirror_lift([z3[p, at, :] for p in range(4)])
        for n in range(2):
            z3[n, at, :] = low[n]
            z3[2 + n, at, :] = high[n]
    for p in range(4):
        s, d = row_lift(z3[p, pl.ds(0, 32, stride=2), :], z3[p, pl.ds(1, 32, stride=2), :])
        r3[p, pl.ds(0, EIGHTH), :] = s[8 : 8 + EIGHTH]
        r3[p, pl.ds(EIGHTH, EIGHTH), :] = d[8 : 8 + EIGHTH]
        for way, part in enumerate(spills(s, d, 8, 24, 3, 4)):
            r3[p, pl.ds(QUARTER + 8 * way, 8), :] = part
            xs[way, pl.ds(N + 8 * p, 8), :] = part

    lane = lax.broadcasted_iota(jnp.int32, (8, N), 1)

    def pack(r, at, to):
        count = r.shape[0]
        wide = N // count
        slot = lane // wide
        to_right, to_left = None, None
        for j in range(count):
            v = r[j, at, :]
            turned = pltpu.roll(v, wide * (j + 1), 1) if j < count - 1 else v
            to_right = turned if j == 0 else jnp.where(slot == j, turned, to_right)
            to_left = turned if j == 0 else jnp.where(slot == (j + 1) % count, turned, to_left)
        ys[0, to, :] = to_right
        ys[1, to, :] = to_left

    def packs(i, _):
        at = pl.ds(pl.multiple_of(8 * i, 8), 8)
        pack(r1, at, at)
        return 0

    lax.fori_loop(0, 16, packs, 0, unroll=2)
    for i in range(8):
        pack(r2, pl.ds(8 * i, 8), pl.ds(N + 8 * i, 8))
    for i in range(4):
        pack(r3, pl.ds(8 * i, 8), pl.ds(N + HALF + 8 * i, 8))
    for way in range(2):
        for level, (r, rows) in enumerate(((r1, N), (r2, HALF), (r3, QUARTER))):
            pack(r, pl.ds(rows + 8 * way, 8), pl.ds(ROWS + SPILL * way + 8 * level, 8))

    pl.semaphore_wait(barrier, len(around))
    own, over, under = pl.ds(0, ROWS), pl.ds(ROWS, SPILL), pl.ds(ROWS + SPILL, SPILL)
    moves = [
        (ys.at[0, under], yr.at[0, over], (down, right)),
        (ys.at[0, over], yr.at[0, under], (up, right)),
        (ys.at[1, under], yr.at[1, over], (down, left)),
        (ys.at[1, over], yr.at[1, under], (up, left)),
        (xs.at[1], xr.at[0], (down, gy)),
        (xs.at[0], xr.at[1], (up, gy)),
        (ys.at[0, own], yr.at[0, own], (gx, right)),
        (ys.at[1, own], yr.at[1, own], (gx, left)),
    ]
    copies = []
    for k, (source, target, device) in enumerate(moves):
        copies.append(
            pltpu.make_async_remote_copy(
                src_ref=source,
                dst_ref=target,
                send_sem=send_sem.at[k],
                recv_sem=recv_sem.at[k],
                device_id=device,
                device_id_type=MESH,
            )
        )
        copies[-1].start()

    for copy in weights:
        copy.wait()

    def plane(p, _):
        own1[p] = product(r1[p, pl.ds(0, N), :], first[OWN], second[OWN])
        return 0

    lax.fori_loop(0, 16, plane, 0)

    def deeper(p, _):
        own2[p] = product(r2[p, pl.ds(0, HALF), :], first[OWN_DEEP], second[OWN_DEEP])
        return 0

    lax.fori_loop(0, 8, deeper, 0)
    out = product(
        jnp.concatenate([r3[p, pl.ds(0, QUARTER), :] for p in range(4)]), first[OWN_DEEP], second[OWN_DEEP]
    )
    own3[...] = out.reshape(4, QUARTER, N)
    for copy in copies:
        copy.wait_recv()
    for copy in copies:
        copy.wait_send()


def exchange(field, first, second):
    f32 = jnp.float32
    shapes = ((16, N, N), (8, HALF, N), (4, QUARTER, N), (2, BLOCKS, N), (2, ROWS + 2 * SPILL, N))
    outs = [jax.ShapeDtypeStruct(shape, f32) for shape in shapes]
    outs += [jax.ShapeDtypeStruct(v.shape, v.dtype) for v in (first, second)]
    return pl.pallas_call(
        exchange_kernel,
        out_shape=tuple(outs),
        in_specs=[pl.BlockSpec(memory_space=pltpu.HBM)] * 3,
        out_specs=(pl.BlockSpec(memory_space=pltpu.VMEM),) * len(outs),
        scratch_shapes=[
            pltpu.VMEM((16, N, N), f32),
            pltpu.VMEM((16, N + 2 * PAD, N), f32),
            pltpu.VMEM((16, N + 16, N), f32),
            pltpu.VMEM((8, HALF + 16, N), f32),
            pltpu.VMEM((4, QUARTER + 16, N), f32),
            pltpu.VMEM((8, N, N), f32),
            pltpu.VMEM((4, HALF, N), f32),
            pltpu.VMEM((2, BLOCKS, N), f32),
            pltpu.VMEM((2, ROWS + 2 * SPILL, N), f32),
            pltpu.SemaphoreType.DMA((6,)),
            pltpu.SemaphoreType.DMA((8,)),
            pltpu.SemaphoreType.DMA((8,)),
        ],
        compiler_params=pltpu.CompilerParams(collective_id=0, has_side_effects=True, vmem_limit_bytes=20 << 20),
        name="exchange",
    )(*[pltpu.with_memory_space_constraint(v, pltpu.HBM) for v in (field, first, second)])


def transform_kernel(
    own1, own2, own3, xr, yr, first, second,
    one_ref, two_ref, three_ref, last_ref, one, two, three, last, fix, across, sem,
):
    f32 = jnp.float32
    sub = lax.broadcasted_iota(jnp.int32, (8, N), 0)
    lane = lax.broadcasted_iota(jnp.int32, (8, N), 1)
    zero = jnp.zeros((8, N), f32)

    def landed(level, over, under):
        low, high, back = ((2, 1, 2), (3, 2, 3), (4, 3, 3))[level]
        return (
            jnp.where(sub < low, over, zero),
            jnp.where(sub >= 8 - back, under, zero),
            jnp.where(sub < high, pltpu.roll(over, 8 - low, 0), zero),
            jnp.where(sub >= 8 - back, pltpu.roll(under, back, 0), zero),
        )

    at = 0
    for level, rows in enumerate((N, HALF, QUARTER)):
        total = None
        for way in range(2):
            over, under = yr[way, pl.ds(ROWS + 8 * level, 8), :], yr[way, pl.ds(ROWS + SPILL + 8 * level, 8), :]
            parts_in = landed(level, over, under)
            pieces, places = [], (0, rows // 2 - 8, rows // 2, rows - 8)
            for r in range(0, rows, 8):
                pieces.append(yr[way, pl.ds(at + r, 8), :])
                for k, place in enumerate(places):
                    if r == place:
                        pieces[-1] = pieces[-1] + parts_in[k]
            weight = REACH + 2 * level + way
            out = product(jnp.concatenate(pieces), first[weight], second[weight])
            total = out if total is None else total + out
        across[pl.ds(at, rows), :] = total
        at += rows
    for way in range(2):
        fix[way, pl.ds(0, HALF), :] = product(xr[way, pl.ds(0, HALF), :], first[OWN], second[OWN])
        fix[way, pl.ds(HALF, BLOCKS - HALF), :] = product(
            xr[way, pl.ds(HALF, BLOCKS - HALF), :], first[OWN_DEEP], second[OWN_DEEP]
        )

    def reached(columns):
        hit = lane == columns[0]
        for column in columns[1:]:
            hit = hit | (lane == column)
        return hit

    def finish(level, own, turned, hit, parts_in, rows, store):
        for k in range(rows // 8):
            v = own(8 * k) + jnp.where(hit, turned[8 * k : 8 * k + 8], zero)
            for part, place in zip(parts_in, (0, rows // 16 - 1, rows // 16, rows // 8 - 1)):
                if k == place:
                    v = v + part
            bx, r = divmod(8 * k, rows // 2)
            store(bx, r, v)

    hit1 = (lane < 2) | (lane >= N - 2) | ((lane >= HALF - 2) & (lane <= HALF))

    def level_one(p, n, turn, bands):
        turned = pltpu.roll(across[pl.ds(0, N), :], lax.rem(2 * N - 2 - 4 * p, N), 1)
        at = pl.ds(pl.multiple_of(8 * n, 8), 8)
        over, under = fix[0, at, :], fix[1, at, :]
        if turn:
            over, under = pltpu.roll(over, 4, 0), pltpu.roll(under, 4, 0)

        def store(bx, r, v):
            if bands[bx] is not None:
                one[bands[bx], n, pl.ds(r, 8), :] = v[:, :HALF]
            one[bands[2 + bx], n, pl.ds(r, 8), :] = pltpu.roll(v, HALF, 1)[:, :HALF]

        finish(0, lambda at: own1[p, pl.ds(at, 8), :], turned, hit1, landed(0, over, under), N, store)

    def low_plane(n, _):
        level_one(n, n, False, (None, 0, 1, 2))
        return 0

    def high_plane(n, _):
        level_one(n + 8, n, True, (3, 4, 5, 6))
        return 0

    outs = [
        pltpu.make_async_copy(one.at[pl.ds(0, 3)], one_ref.at[pl.ds(0, 3)], sem.at[0]),
        pltpu.make_async_copy(one.at[pl.ds(3, 4)], one_ref.at[pl.ds(3, 4)], sem.at[1]),
        pltpu.make_async_copy(two, two_ref, sem.at[2]),
        pltpu.make_async_copy(three, three_ref, sem.at[3]),
        pltpu.make_async_copy(last, last_ref, sem.at[4]),
    ]
    lax.fori_loop(0, 8, high_plane, 0)
    outs[1].start()
    lax.fori_loop(0, 8, low_plane, 0)
    outs[0].start()

    def deeper(level, count, rows, at, block, own, columns, bases, size, out, corner):
        hit = reached(columns)
        wide = N // count
        for p in range(count):
            turned = across[pl.ds(at, rows), :]
            if p:
                turned = pltpu.roll(turned, N - wide * p, 1)
            here = pl.ds(block + 8 * p, 8)
            bz, n = divmod(p, count // 2)

            def store(bx, r, v):
                for by in range(2):
                    band = 4 * bz + 2 * by + bx
                    part = v[:, bases[by] : bases[by] + size]
                    if band:
                        out[band - 1, n, pl.ds(r, 8), :] = part
                    elif corner is not None:
                        corner[n, pl.ds(r, 8), :] = part

            finish(level, lambda at: own[p, pl.ds(at, 8), :], turned, hit, landed(level, fix[0, here, :], fix[1, here, :]), rows, store)

    deeper(1, 8, HALF, N, HALF, own2, columns_two(), (0, HIGH2), QUARTER, two, None)
    outs[2].start()
    deeper(2, 4, QUARTER, N + HALF, N, own3, columns_three(), (LOW3, HIGH3), EIGHTH, three, last)
    outs[3].start()
    outs[4].start()
    for copy in outs:
        copy.wait()


def transform(*arrays):
    f32 = jnp.float32
    shapes = ((7, 8, HALF, HALF), (7, 4, QUARTER, QUARTER), (7, 2, EIGHTH, EIGHTH), (2, EIGHTH, EIGHTH))
    return pl.pallas_call(
        transform_kernel,
        out_shape=tuple(jax.ShapeDtypeStruct(shape, f32) for shape in shapes),
        in_specs=[pl.BlockSpec(memory_space=pltpu.VMEM)] * len(arrays),
        out_specs=(pl.BlockSpec(memory_space=pltpu.HBM),) * 4,
        scratch_shapes=[pltpu.VMEM(shape, f32) for shape in shapes]
        + [
            pltpu.VMEM((2, BLOCKS, N), f32),
            pltpu.VMEM((ROWS, N), f32),
            pltpu.SemaphoreType.DMA((5,)),
        ],
        compiler_params=pltpu.CompilerParams(vmem_limit_bytes=20 << 20),
        name="transform",
    )(*arrays)


def shards(ocean_field):
    first, second = paired(lane_filters())
    return transform(*exchange(ocean_field, jnp.asarray(first), jnp.asarray(second)))


def solution(mesh):
    return jax.shard_map(
        shards,
        mesh=mesh,
        in_specs=(P(None, "gx", "gy"),),
        out_specs=(
            P(None, None, "gx", "gy"),
            P(None, None, "gx", "gy"),
            P(None, None, "gx", "gy"),
            P(None, "gx", "gy"),
        ),
        check_vma=False,
    )
```

time: 23 us -> 19.1 us (0.83)
  Pallas kernels: 22.3 us -> 18.4 us
    pallas_call x1, Pallas kernels: 16.7 us -> 14 us  [exchange(): pl.pallas_call(exchange_kernel, out_shape=tuple(outs), in_specs=[pl.Block...]
    pallas_call x1, Pallas kernels: 5.58 us -> 4.42 us  [transform(): pl.pallas_call(transform_kernel, out_shape=tuple((jax.ShapeDtypeStruct(sh...]
where the time goes in v3:
time: 19.1 us; the launch traced here: 19 us
  Pallas kernels  18.4 us (96%)
  between operations  0.64 us (3%)
    pallas_call x1, Pallas kernels, exchange(): pl.pallas_call(exchange_kernel, out_shape=tuple(outs), in_specs=[pl.Block...  14 us
    pallas_call x1, Pallas kernels, transform(): pl.pallas_call(transform_kernel, out_shape=tuple((jax.ShapeDtypeStruct(sh...  4.42 us

profile of v3, /device:TPU:1, one launch (start us, length us, event | category | flops | bytes accessed | tf_op | source)
XLA Modules:
  0.0 19.0 jit_solution(9881939273124062349)
XLA Ops:
  0.6 14.0 %exchange.1 = (f32[16,128,128]{2,1,0:T(8,128)S(1)}, f32[8,64,128]{2,1,0:T(8,128)S(1)}, f32[4,32,128]{2,1,0:T(8,128)S(1)}, f32[2,160,128]{2,1,0:T(8,128)S(1)}, f3...) custom-call(f32[16,128,128]{2,1,0:T(8,128)} %x_ref.1, ...), custom_call_target="tpu_custom_call" | custom-call | tf_op jit(solution)/shard_map/exchange/pallas_call | solution.py:305
  14.6 4.4 %transform.1 = (f32[7,8,64,64]{3,2,1,0:T(8,128)}, f32[7,4,32,32]{3,2,1,0:T(8,128)}, f32[7,2,16,16]{3,2,1,0:T(8,128)}, f32[2,16,16]{2,1,0:T(8,128)}) custom-call(f32[16,128,128]{2,1,0:T(8,128)S(1)} %get-tuple-element.11.own1, f32[8,64,128]{2,1,0:T(8,128)S(1)} %get-tuple-element.12.own2, f32[4,32,128]{2,1,0:T(8,128)S(1)} %get-tuple-element.13.own3, ...), custom_call_target="tpu_custom_call" | custom-call | tf_op jit(solution)/shard_map/transform/pallas_call | solution.py:454
